TPU v7x, 128 devices: a whole 4x4x4 slice. The times are simulated.
128 devices in a mesh: dp: 8 (over z, core), mp: 16 (over x, y).
Axes of the slice: x: 4, y: 4, z: 4, core: 2. Of those that a mesh axis runs over, the one named last changes fastest.
Arguments:
- activations: bfloat16 [16384, 5120], P(('dp', 'mp')), may hold values from -10 to 10
- cotangent: bfloat16 [16384, 5120], P('dp', 'mp'), may hold values from -1 to 1
- master_weights: float32 [5120, 5120], P('dp', 'mp'), may hold values from -32 to 32
- first_moment: float32 [5120, 5120], P('dp', 'mp'), may hold values from -1 to 1
- second_moment: float32 [5120, 5120], P('dp', 'mp'), may hold values from 0.25 to 4
- step_count: int32 [1], replicated, may hold values from 1 to 23
- language_ids: int32 [1], replicated, may hold values from 0 to 7
- language_rates: float32 [8], replicated, may hold values from 0.25 to 2
Outputs:
- new_master: float32 [5120, 5120], P('dp', 'mp')
- new_first: float32 [5120, 5120], P('dp', 'mp')
- new_second: float32 [5120, 5120], P('dp', 'mp')
- new_weights: bfloat16 [5120, 5120], P(None, 'mp')
All inputs are finite; a program needn't handle non-finite values.
Results may differ from a plain program's by a relative error of at most 0.0004.
Values may be sent and summed in bfloat16 or wider, within the bound.
No kernel may reach another device: no remote copies, remote signals or barrier semaphores. Data moves between devices by JAX's collectives and lax.ppermute only.
A program may use at most 128 MiB of HBM per device.

v0:
```python
import jax
import jax.numpy as jnp
from jax import lax
from jax.sharding import PartitionSpec as P

beta_one = 0.9
beta_two = 0.999
epsilon = 1e-06
decay_weight = 0.1
base_rate = 0.25


def on_device(
    activations,
    cotangent,
    master_weights,
    first_moment,
    second_moment,
    step_count,
    language_ids,
    language_rates,
):
    gathered = lax.all_gather(activations, "mp", axis=0, tiled=True)
    gradient = lax.psum_scatter(
        lax.dot_general(
            gathered, cotangent, (((0,), (0,)), ((), ())), preferred_element_type=jnp.float32
        ),
        "dp",
        scatter_dimension=0,
        tiled=True,
    )
    steps_done = step_count[0].astype(jnp.float32)
    corr_one = 1.0 - jnp.power(jnp.float32(beta_one), steps_done)
    corr_two = 1.0 - jnp.power(jnp.float32(beta_two), steps_done)
    new_first = beta_one * first_moment + (1.0 - beta_one) * gradient
    new_second = beta_two * second_moment + (1.0 - beta_two) * gradient * gradient
    update = (
        new_first / corr_one / (jnp.sqrt(new_second / corr_two) + epsilon)
        + decay_weight * master_weights
    )
    weight_sq, update_sq = lax.psum(
        (jnp.sum(master_weights * master_weights), jnp.sum(update * update)), ("dp", "mp")
    )
    trust = jnp.sqrt(weight_sq) / jnp.sqrt(update_sq)
    picked = jnp.arange(language_rates.shape[0], dtype=jnp.int32) == language_ids[0]
    rate = base_rate * jnp.sum(jnp.where(picked, language_rates, jnp.float32(0.0)))
    new_master = master_weights - rate * trust * update
    new_weights = lax.all_gather(new_master.astype(jnp.bfloat16), "dp", axis=0, tiled=True)
    return (new_master, new_first, new_second, new_weights)


def solution(mesh):
    return jax.shard_map(
        on_device,
        mesh=mesh,
        in_specs=(
            P(("dp", "mp"), None),
            P("dp", "mp"),
            P("dp", "mp"),
            P("dp", "mp"),
            P("dp", "mp"),
            P(),
            P(),
            P(),
        ),
        out_specs=(P("dp", "mp"), P("dp", "mp"), P("dp", "mp"), P(None, "mp")),
        check_vma=False,
    )
```

profile of v0, /device:TPU:1, one launch (start us, length us, event | category | flops | bytes accessed | tf_op | source)
XLA Modules:
  0.0 311.8 jit_solution(5477487466860797035)
XLA Ops:
  7.2 0.0 copy-start
  7.2 0.0 all-gather.3.cloned.1.call-start
  7.2 0.7 all-gather.3.cloned.1.call-update
  7.9 0.0 reduce-scatter.2.cloned.1.call-start
  8.0 138.1 %all-gather.3.cloned.1.call-done = bf16[2048,5120]{1,0:T(8,128)(2,1)} async-done(((bf16[128,5120]{1,0:T(8,128)(2,1)}), bf16[2048,5120]{1,0:T(8,128)(2,1)}) %all-gather.3.cloned.1.call-update) | async-done | bytes 20971536 | tf_op jit(solution)/shard_map/all_gather | solution.py:23
  146.0 0.0 copy-done
  146.0 13.9 %fusion.4 = f32[5120,320]{0,1:T(8,128)} fusion(bf16[2048,320]{0,1:T(8,128)(2,1)S(1)} %copy-done, bf16[2048,5120]{1,0:T(8,128)(2,1)} %all-gather.3.cloned.1.call-done), kind=kOutput, calls=%fused_computation.10 | convolution fusion | flops 6710886400 | bytes 28835840 | tf_op jit(solution)/shard_map/dot_general | solution.py:25
  159.9 0.0 copy-start.2
  159.9 0.0 copy-start.1
  159.9 0.0 reduce-scatter.2.cloned.1.call-update
  160.0 0.0 all-gather.5.cloned.1.call-start
  161.5 0.0 copy-done.2
  161.5 0.6 fusion.1
  162.7 40.4 %reduce-scatter.2.cloned.1.call-done = f32[640,320]{0,1:T(8,128)} async-done(((f32[5120,320]{0,1:T(8,128)}), f32[640,320]{0,1:T(8,128)}) %reduce-scatter.2.cloned.1.call-update) | async-done | bytes 819216 | tf_op jit(solution)/shard_map/reduce_scatter | solution.py:24
  203.1 0.0 copy-done.1
  203.1 4.1 %multiply_reduce_fusion = (f32[]{:T(128)}, f32[640,320]{0,1:T(8,128)S(1)}, f32[640,320]{0,1:T(8,128)}, f32[640,320]{0,1:T(8,128)}, f32[]{:T(128)}) fusion(f32[640,320]{0,1:T(8,128)S(1)} %copy-done.1, f32[]{:T(128)} %bitcast.2, f32[]{:T(128)} %bitcast.1, f32[640,320]{0,1:T(8,128)} %reduce-scatter.2.cloned.1.call-done, f32[640,320]{0,1:T(8,128)} %param.12, ...), kind=kLoop, calls=%fused_computation.3 | loop fusion | flops 3481598 | bytes 5734416 | tf_op jit(solution)/shard_map/reduce_sum | solution.py:42
  207.2 66.1 %all-reduce = (f32[]{:T(128)}, f32[]{:T(128)}) all-reduce(f32[]{:T(128)} %get-tuple-element.12, f32[]{:T(128)} %get-tuple-element.8), channel_id=1, replica_groups=mesh['dp'=8,'mp'=16] {'dp','mp'}, use_global_device_ids=true, to_apply=%region_2.0 | all-reduce | flops 2 | bytes 16 | tf_op jit(solution)/shard_map/psum | solution.py:41
  274.7 1.1 fusion.2
  275.8 0.0 all-gather.5.cloned.1.call-update
  275.8 25.6 %all-gather.5.cloned.1.call-done = bf16[5120,320]{0,1:T(8,128)(2,1)} async-done(((bf16[640,320]{0,1:T(8,128)(2,1)}), bf16[5120,320]{0,1:T(8,128)(2,1)}) %all-gather.5.cloned.1.call-update) | async-done | bytes 3276816 | tf_op jit(solution)/shard_map/all_gather | solution.py:48
  301.4 3.8 %copy.15 = bf16[5120,320]{0,1:T(8,128)(2,1)} copy(bf16[5120,320]{0,1:T(8,128)(2,1)} %all-gather.5.cloned.1.call-done) | data formatting | bytes 6553600
Async XLA Ops:
  7.2 138.9 %copy-start = (bf16[2048,320]{0,1:T(8,128)(2,1)S(1)}, bf16[2048,320]{0,1:T(8,128)(2,1)}, u32[]{:S(2)}) copy-start(bf16[2048,320]{0,1:T(8,128)(2,1)} %param.9) | copy-start | bytes 3932164
  7.2 138.9 %all-gather.3.cloned.1.call-start = ((), (), s32[]{:S(2)}) async-start(), calls=%async_computation.1 | async-start | bytes 22282240 | tf_op jit(solution)/shard_map/all_gather | solution.py:23
  7.9 195.2 %reduce-scatter.2.cloned.1.call-start = ((), (), s32[]{:S(2)}) async-start(), calls=%async_computation.2 | async-start | bytes 7372800 | tf_op jit(solution)/shard_map/reduce_scatter | solution.py:24
  159.9 1.5 copy-start.2
  159.9 43.2 %copy-start.1 = (f32[640,320]{0,1:T(8,128)S(1)}, f32[640,320]{0,1:T(8,128)}, u32[]{:S(2)}) copy-start(f32[640,320]{0,1:T(8,128)} %param.10) | copy-start | bytes 2457604
  160.0 141.4 %all-gather.5.cloned.1.call-start = ((), (), s32[]{:S(2)}) async-start(), calls=%async_computation.3 | async-start | bytes 3686400 | tf_op jit(solution)/shard_map/all_gather | solution.py:48
Sparse Core Ops, SparseCore 0:
  10.2 135.8 all-gather.2
  160.1 42.9 reduce-scatter.1
  276.0 25.3 all-gather.4
where the time goes:
time: 312 us
  waiting for transfers between devices  205 us (66%)
  blocking collectives  66.1 us (21%)
  between operations  17.2 us (6%)
  matrix products  13.9 us (4%)
  other arithmetic  5.83 us (2%)
  local copies, waits for them, and re-layouts  3.86 us (1%)
    all_gather x1, waiting for transfers between devices, on_device(): gathered = lax.all_gather(activations, 'mp', axis=0, tiled=True)  138 us
    psum x1, blocking collectives, on_device(): lax.psum((jnp.sum(master_weights * master_weights), jnp.sum(update * upda...  66.1 us
    reduce_scatter x1, waiting for transfers between devices, on_device(): lax.psum_scatter(lax.dot_general(gathered, cotangent, (((0,), (0,)), ((),...  40.4 us
    all_gather x1, waiting for transfers between devices, on_device(): lax.all_gather(new_master.astype(jnp.bfloat16), 'dp', axis=0, tiled=True)  25.6 us
    dot_general x1, matrix products, on_device(): lax.dot_general(gathered, cotangent, (((0,), (0,)), ((), ())), preferred_...  13.9 us
  transfers between devices with their start and end apart: 3, of which 3 were waited for; matrix products, arithmetic and copies ran while one was open for 0% of the time, Pallas kernels for 0%

commit v1 on v0

--- a/solution.py
+++ b/solution.py
@@ -10,6 +10,22 @@
 base_rate = 0.25
 
 
+def gather_around(x, axis, dim):
+    ways, here, step = (lax.axis_size(axis), lax.axis_index(axis), x.shape[dim])
+    shape = [n * ways if d == dim else n for d, n in enumerate(x.shape)]
+    full = lax.dynamic_update_slice_in_dim(jnp.zeros(shape, x.dtype), x, here * step, axis=dim)
+    going_up = going_down = x
+    for far in range(1, ways // 2 + 1):
+        going_up = lax.ppermute(going_up, axis, [(d, (d + 1) % ways) for d in range(ways)])
+        full = lax.dynamic_update_slice_in_dim(full, going_up, (here - far) % ways * step, axis=dim)
+        if 2 * far < ways:
+            going_down = lax.ppermute(going_down, axis, [(d, (d - 1) % ways) for d in range(ways)])
+            full = lax.dynamic_update_slice_in_dim(
+                full, going_down, (here + far) % ways * step, axis=dim
+            )
+    return full
+
+
 def on_device(
     activations,
     cotangent,
@@ -20,7 +36,7 @@
     language_ids,
     language_rates,
 ):
-    gathered = lax.all_gather(activations, "mp", axis=0, tiled=True)
+    gathered = gather_around(activations, "mp", 0)
     gradient = lax.psum_scatter(
         lax.dot_general(
             gathered, cotangent, (((0,), (0,)), ((), ())), preferred_element_type=jnp.float32

time: 312 us -> 422 us (1.35)
  starting transfers between devices: 0.12 us -> 37.5 us
  local copies, waits for them, and re-layouts: 3.86 us -> 40.1 us
  waiting for transfers between devices: 205 us -> 240 us
    ppermute x0 -> x15, waiting for transfers between devices: none -> 170 us  [the longest x8 147 us: gather_around(): lax.ppermute(going_up, axis, [(d, (d + 1) % ways) for d in range(ways)])]
    all_gather x1 -> x0, waiting for transfers between devices: 138 us -> none  [on_device(): gathered = lax.all_gather(activations, 'mp', axis=0, tiled=True)]
    ppermute x0 -> x15, starting transfers between devices: none -> 37.4 us  [the longest x7 35.2 us: gather_around(): lax.ppermute(going_down, axis, [(d, (d - 1) % ways) for d in range(ways)])]
    dynamic_update_slice x0 -> x16, local copies, waits for them, and re-layouts: none -> 27.8 us  [the longest x8 14.5 us: gather_around(): lax.dynamic_update_slice_in_dim(full, going_up, (here - far) % ways * ste...]
    broadcast_in_dim x0 -> x1, local copies, waits for them, and re-layouts: none -> 7.36 us  [gather_around(): jnp.zeros(shape, x.dtype)]
  transfers between devices with their start and end apart: 3 -> 17, of which waited for: 3 -> 14; matrix products, arithmetic and copies ran while one was open for 0% -> 8% of each run, Pallas kernels for 0% -> 0%
where the time goes in v1:
time: 422 us; the launch traced here: 421 us
  waiting for transfers between devices  240 us (57%)
  blocking collectives  66.1 us (16%)
  local copies, waits for them, and re-layouts  40.1 us (10%)
  starting transfers between devices  37.5 us (9%)
  between operations  17.5 us (4%)
  matrix products  14 us (3%)
  other arithmetic  5.83 us (1%)
    ppermute x8, waiting for transfers between devices, gather_around(): lax.ppermute(going_up, axis, [(d, (d + 1) % ways) for d in range(ways)])  147 us
    psum x1, blocking collectives, on_device(): lax.psum((jnp.sum(master_weights * master_weights), jnp.sum(update * upda...  66.1 us
    reduce_scatter x1, waiting for transfers between devices, on_device(): lax.psum_scatter(lax.dot_general(gathered, cotangent, (((0,), (0,)), ((),...  44.4 us
    ppermute x7, starting transfers between devices, gather_around(): lax.ppermute(going_down, axis, [(d, (d - 1) % ways) for d in range(ways)])  35.2 us
    all_gather x1, waiting for transfers between devices, on_device(): lax.all_gather(new_master.astype(jnp.bfloat16), 'dp', axis=0, tiled=True)  25.6 us
    ppermute x7, waiting for transfers between devices, gather_around(): lax.ppermute(going_down, axis, [(d, (d - 1) % ways) for d in range(ways)])  22.7 us
    dynamic_update_slice x8, local copies, waits for them, and re-layouts, gather_around(): lax.dynamic_update_slice_in_dim(full, going_up, (here - far) % ways * ste...  14.5 us
    dot_general x1, matrix products, on_device(): lax.dot_general(gathered, cotangent, (((0,), (0,)), ((), ())), preferred_...  14 us
  transfers between devices with their start and end apart: 17, of which 14 were waited for; matrix products, arithmetic and copies ran while one was open for 8% of the time, Pallas kernels for 0%

profile of v1, /device:TPU:1, one launch (start us, length us, event | category | flops | bytes accessed | tf_op | source)
XLA Modules:
  0.0 421.2 jit_solution(16422306052630820339)
XLA Ops:
  9.4 3.7 collective-permute-start.1
  13.1 28.6 %collective-permute-done = bf16[128,5120]{1,0:T(8,128)(2,1)S(1)} collective-permute-done((bf16[128,5120]{1,0:T(8,128)(2,1)}, bf16[128,5120]{1,0:T(8,128)(2,1)S(1)}, u32[]{:S(2)}, u32[]{:S(2)}) %collective-permute-start) | collective-permute-done | bytes 1310752 | tf_op jit(solution)/shard_map/ppermute | solution.py:19
  42.8 4.7 %collective-permute-start.3 = (bf16[128,5120]{1,0:T(8,128)(2,1)S(1)}, bf16[128,5120]{1,0:T(8,128)(2,1)}, u32[]{:S(2)}, u32[]{:S(2)}) collective-permute-start(bf16[128,5120]{1,0:T(8,128)(2,1)S(1)} %collective-permute-done.1), channel_id=1, source_target_pairs={{0,15},{1,0},{2,1},{3,2},{4,3},{5,4},{6,5},{7,6},{8,7},{9,8},{10,9... | collective-permute-start | bytes 3932168 | tf_op jit(solution)/shard_map/ppermute | solution.py:22
  47.6 26.6 %collective-permute-done.2 = bf16[128,5120]{1,0:T(8,128)(2,1)} collective-permute-done((bf16[128,5120]{1,0:T(8,128)(2,1)S(1)}, bf16[128,5120]{1,0:T(8,128)(2,1)}, u32[]{:S(2)}, u32[]{:S(2)}) %collective-permute-start.2) | collective-permute-done | bytes 1310752 | tf_op jit(solution)/shard_map/ppermute | solution.py:19
  74.1 5.6 %collective-permute-start.5 = (bf16[128,5120]{1,0:T(8,128)(2,1)}, bf16[128,5120]{1,0:T(8,128)(2,1)}, u32[]{:S(2)}, u32[]{:S(2)}) collective-permute-start(bf16[128,5120]{1,0:T(8,128)(2,1)} %collective-permute-done.3), channel_id=1, source_target_pairs={{0,15},{1,0},{2,1},{3,2},{4,3},{5,4},{6,5},{7,6},{8,7},{9,8},{10,9... | collective-permute-start | bytes 3932168 | tf_op jit(solution)/shard_map/ppermute | solution.py:22
  79.7 26.1 %collective-permute-done.4 = bf16[128,5120]{1,0:T(8,128)(2,1)} collective-permute-done((bf16[128,5120]{1,0:T(8,128)(2,1)}, bf16[128,5120]{1,0:T(8,128)(2,1)}, u32[]{:S(2)}, u32[]{:S(2)}) %collective-permute-start.4) | collective-permute-done | bytes 1310752 | tf_op jit(solution)/shard_map/ppermute | solution.py:19
  105.8 7.4 %broadcast_in_dim.8 = bf16[2048,5120]{1,0:T(8,128)(2,1)} broadcast(bf16[]{:T(256)} %constant.106.clone.1), dimensions={} | broadcast | bytes 20971522 | tf_op jit(solution)/shard_map/broadcast_in_dim | solution.py:16
  114.4 2.5 constant_dynamic-update-slice_fusion.14
  116.8 4.8 %collective-permute-start.7 = (bf16[128,5120]{1,0:T(8,128)(2,1)}, bf16[128,5120]{1,0:T(8,128)(2,1)S(1)}, u32[]{:S(2)}, u32[]{:S(2)}) collective-permute-start(bf16[128,5120]{1,0:T(8,128)(2,1)} %collective-permute-done.5), channel_id=1, source_target_pairs={{0,15},{1,0},{2,1},{3,2},{4,3},{5,4},{6,5},{7,6},{8,7},{9,8},{10,9... | collective-permute-start | bytes 3932168 | tf_op jit(solution)/shard_map/ppermute | solution.py:22
  121.6 2.5 constant_dynamic-update-slice_fusion.13
  124.1 12.5 %collective-permute-done.6 = bf16[128,5120]{1,0:T(8,128)(2,1)} collective-permute-done((bf16[128,5120]{1,0:T(8,128)(2,1)}, bf16[128,5120]{1,0:T(8,128)(2,1)}, u32[]{:S(2)}, u32[]{:S(2)}) %collective-permute-start.6) | collective-permute-done | bytes 1310752 | tf_op jit(solution)/shard_map/ppermute | solution.py:19
  136.6 2.5 constant_dynamic-update-slice_fusion.12
  139.1 2.5 constant_dynamic-update-slice_fusion.11
  141.5 5.1 %collective-permute-done.7 = bf16[128,5120]{1,0:T(8,128)(2,1)S(1)} collective-permute-done((bf16[128,5120]{1,0:T(8,128)(2,1)}, bf16[128,5120]{1,0:T(8,128)(2,1)S(1)}, u32[]{:S(2)}, u32[]{:S(2)}) %collective-permute-start.7) | collective-permute-done | bytes 1310752 | tf_op jit(solution)/shard_map/ppermute | solution.py:22
  146.6 5.4 %collective-permute-start.9 = (bf16[128,5120]{1,0:T(8,128)(2,1)S(1)}, bf16[128,5120]{1,0:T(8,128)(2,1)S(1)}, u32[]{:S(2)}, u32[]{:S(2)}) collective-permute-start(bf16[128,5120]{1,0:T(8,128)(2,1)S(1)} %collective-permute-done.7), channel_id=1, source_target_pairs={{0,15},{1,0},{2,1},{3,2},{4,3},{5,4},{6,5},{7,6},{8,7},{9,8},{10,9... | collective-permute-start | bytes 3932168 | tf_op jit(solution)/shard_map/ppermute | solution.py:22
  152.0 2.5 constant_dynamic-update-slice_fusion.10
  154.5 11.9 %collective-permute-done.8 = bf16[128,5120]{1,0:T(8,128)(2,1)S(1)} collective-permute-done((bf16[128,5120]{1,0:T(8,128)(2,1)}, bf16[128,5120]{1,0:T(8,128)(2,1)S(1)}, u32[]{:S(2)}, u32[]{:S(2)}) %collective-permute-start.8) | collective-permute-done | bytes 1310752 | tf_op jit(solution)/shard_map/ppermute | solution.py:19
  168.8 2.5 constant_dynamic-update-slice_fusion.8
  171.3 4.5 %collective-permute-done.9 = bf16[128,5120]{1,0:T(8,128)(2,1)S(1)} collective-permute-done((bf16[128,5120]{1,0:T(8,128)(2,1)S(1)}, bf16[128,5120]{1,0:T(8,128)(2,1)S(1)}, u32[]{:S(2)}, u32[]{:S(2)}) %collective-permute-start.9) | collective-permute-done | bytes 1310752 | tf_op jit(solution)/shard_map/ppermute | solution.py:22
  175.8 5.5 %collective-permute-start.11 = (bf16[128,5120]{1,0:T(8,128)(2,1)S(1)}, bf16[128,5120]{1,0:T(8,128)(2,1)S(1)}, u32[]{:S(2)}, u32[]{:S(2)}) collective-permute-start(bf16[128,5120]{1,0:T(8,128)(2,1)S(1)} %collective-permute-done.9), channel_id=1, source_target_pairs={{0,15},{1,0},{2,1},{3,2},{4,3},{5,4},{6,5},{7,6},{8,7},{9,8},{10,9... | collective-permute-start | bytes 3932168 | tf_op jit(solution)/shard_map/ppermute | solution.py:22
  182.5 12.5 %collective-permute-done.10 = bf16[128,5120]{1,0:T(8,128)(2,1)S(1)} collective-permute-done((bf16[128,5120]{1,0:T(8,128)(2,1)S(1)}, bf16[128,5120]{1,0:T(8,128)(2,1)S(1)}, u32[]{:S(2)}, u32[]{:S(2)}) %collective-permute-start.10) | collective-permute-done | bytes 1310752 | tf_op jit(solution)/shard_map/ppermute | solution.py:19
  197.3 6.8 %collective-permute-done.11 = bf16[128,5120]{1,0:T(8,128)(2,1)S(1)} collective-permute-done((bf16[128,5120]{1,0:T(8,128)(2,1)S(1)}, bf16[128,5120]{1,0:T(8,128)(2,1)S(1)}, u32[]{:S(2)}, u32[]{:S(2)}) %collective-permute-start.11) | collective-permute-done | bytes 1310752 | tf_op jit(solution)/shard_map/ppermute | solution.py:22
  204.1 5.5 %collective-permute-start.13 = (bf16[128,5120]{1,0:T(8,128)(2,1)S(1)}, bf16[128,5120]{1,0:T(8,128)(2,1)S(1)}, u32[]{:S(2)}, u32[]{:S(2)}) collective-permute-start(bf16[128,5120]{1,0:T(8,128)(2,1)S(1)} %collective-permute-done.11), channel_id=1, source_target_pairs={{0,15},{1,0},{2,1},{3,2},{4,3},{5,4},{6,5},{7,6},{8,7},{9,8},{10,9... | collective-permute-start | bytes 3932168 | tf_op jit(solution)/shard_map/ppermute | solution.py:22
  210.8 11.9 %collective-permute-done.12 = bf16[128,5120]{1,0:T(8,128)(2,1)S(1)} collective-permute-done((bf16[128,5120]{1,0:T(8,128)(2,1)S(1)}, bf16[128,5120]{1,0:T(8,128)(2,1)S(1)}, u32[]{:S(2)}, u32[]{:S(2)}) %collective-permute-start.12) | collective-permute-done | bytes 1310752 | tf_op jit(solution)/shard_map/ppermute | solution.py:19
  225.1 6.4 %collective-permute-done.13 = bf16[128,5120]{1,0:T(8,128)(2,1)S(1)} collective-permute-done((bf16[128,5120]{1,0:T(8,128)(2,1)S(1)}, bf16[128,5120]{1,0:T(8,128)(2,1)S(1)}, u32[]{:S(2)}, u32[]{:S(2)}) %collective-permute-start.13) | collective-permute-done | bytes 1310752 | tf_op jit(solution)/shard_map/ppermute | solution.py:22
  232.7 17.3 %collective-permute-done.14 = bf16[128,5120]{1,0:T(8,128)(2,1)S(1)} collective-permute-done((bf16[128,5120]{1,0:T(8,128)(2,1)S(1)}, bf16[128,5120]{1,0:T(8,128)(2,1)S(1)}, u32[]{:S(2)}, u32[]{:S(2)}) %collective-permute-start.14) | collective-permute-done | bytes 1310752 | tf_op jit(solution)/shard_map/ppermute | solution.py:19
  251.1 14.0 %fusion.4 = f32[5120,320]{0,1:T(8,128)} fusion(bf16[2048,320]{0,1:T(8,128)(2,1)S(1)} %copy-done, bf16[2048,5120]{1,0:T(8,128)(2,1)} %constant_dynamic-update-slice_fusion), kind=kOutput, calls=%fused_computation.26 | convolution fusion | flops 6710886400 | bytes 28835840 | tf_op jit(solution)/shard_map/dot_general | solution.py:41
  267.8 44.4 %reduce-scatter.2.cloned.1.call-done = f32[640,320]{0,1:T(8,128)} async-done(((f32[5120,320]{0,1:T(8,128)}), f32[640,320]{0,1:T(8,128)}) %reduce-scatter.2.cloned.1.call-update) | async-done | bytes 819216 | tf_op jit(solution)/shard_map/reduce_scatter | solution.py:40
  312.2 4.1 multiply_reduce_fusion
  316.3 66.1 %all-reduce = (f32[]{:T(128)}, f32[]{:T(128)}) all-reduce(f32[]{:T(128)} %get-tuple-element.12, f32[]{:T(128)} %get-tuple-element.8), channel_id=1, replica_groups=mesh['dp'=8,'mp'=16] {'dp','mp'}, use_global_device_ids=true, to_apply=%region_2.3 | all-reduce | flops 2 | bytes 16 | tf_op jit(solution)/shard_map/psum | solution.py:57
  384.9 25.6 %all-gather.2.cloned.1.call-done = bf16[5120,320]{0,1:T(8,128)(2,1)} async-done(((bf16[640,320]{0,1:T(8,128)(2,1)}), bf16[5120,320]{0,1:T(8,128)(2,1)}) %all-gather.2.cloned.1.call-update) | async-done | bytes 3276816 | tf_op jit(solution)/shard_map/all_gather | solution.py:64
  410.5 3.8 copy.31
  (39 shorter events, 18.1 us)
Async XLA Ops:
  7.2 243.9 %copy-start = (bf16[2048,320]{0,1:T(8,128)(2,1)S(1)}, bf16[2048,320]{0,1:T(8,128)(2,1)}, u32[]{:S(2)}) copy-start(bf16[2048,320]{0,1:T(8,128)(2,1)} %param.9) | copy-start | bytes 3932164
  7.2 106.0 %copy-start.2 = (bf16[128,5120]{1,0:T(8,128)(2,1)S(1)}, bf16[128,5120]{1,0:T(8,128)(2,1)}, u32[]{:S(2)}) copy-start(bf16[128,5120]{1,0:T(8,128)(2,1)} %param.8) | copy-start | bytes 3932164
  7.2 305.0 %reduce-scatter.2.cloned.1.call-start = ((), (), s32[]{:S(2)}) async-start(), calls=%async_computation.1 | async-start | bytes 7372800 | tf_op jit(solution)/shard_map/reduce_scatter | solution.py:40
  7.2 34.5 %collective-permute-start = (bf16[128,5120]{1,0:T(8,128)(2,1)}, bf16[128,5120]{1,0:T(8,128)(2,1)S(1)}, u32[]{:S(2)}, u32[]{:S(2)}) collective-permute-start(bf16[128,5120]{1,0:T(8,128)(2,1)} %param.8), channel_id=1, source_target_pairs={{0,1},{1,2},{2,3},{3,4},{4,5},{5,6},{6,7},{7,8},{8,9},{9,10},{10,1... | collective-permute-start | bytes 3932168 | tf_op jit(solution)/shard_map/ppermute | solution.py:19
  9.4 32.3 %collective-permute-start.1 = (bf16[128,5120]{1,0:T(8,128)(2,1)}, bf16[128,5120]{1,0:T(8,128)(2,1)S(1)}, u32[]{:S(2)}, u32[]{:S(2)}) collective-permute-start(bf16[128,5120]{1,0:T(8,128)(2,1)} %param.8), channel_id=1, source_target_pairs={{0,15},{1,0},{2,1},{3,2},{4,3},{5,4},{6,5},{7,6},{8,7},{9,8},{10,9... | collective-permute-start | bytes 3932168 | tf_op jit(solution)/shard_map/ppermute | solution.py:22
  41.7 32.4 %copy-start.4 = (bf16[128,5120]{1,0:T(8,128)(2,1)}, bf16[128,5120]{1,0:T(8,128)(2,1)S(1)}, u32[]{:S(2)}) copy-start(bf16[128,5120]{1,0:T(8,128)(2,1)S(1)} %collective-permute-done) | copy-start | bytes 3932164
  41.7 32.4 %collective-permute-start.2 = (bf16[128,5120]{1,0:T(8,128)(2,1)S(1)}, bf16[128,5120]{1,0:T(8,128)(2,1)}, u32[]{:S(2)}, u32[]{:S(2)}) collective-permute-start(bf16[128,5120]{1,0:T(8,128)(2,1)S(1)} %collective-permute-done), channel_id=1, source_target_pairs={{0,1},{1,2},{2,3},{3,4},{4,5},{5,6},{6,7},{7,8},{8,9},{9,10},{10,1... | collective-permute-start | bytes 3932168 | tf_op jit(solution)/shard_map/ppermute | solution.py:19
  41.7 1.1 copy-start.3
  42.8 31.3 %collective-permute-start.3 = (bf16[128,5120]{1,0:T(8,128)(2,1)S(1)}, bf16[128,5120]{1,0:T(8,128)(2,1)}, u32[]{:S(2)}, u32[]{:S(2)}) collective-permute-start(bf16[128,5120]{1,0:T(8,128)(2,1)S(1)} %collective-permute-done.1), channel_id=1, source_target_pairs={{0,15},{1,0},{2,1},{3,2},{4,3},{5,4},{6,5},{7,6},{8,7},{9,8},{10,9... | collective-permute-start | bytes 3932168 | tf_op jit(solution)/shard_map/ppermute | solution.py:22
  74.1 31.7 %collective-permute-start.4 = (bf16[128,5120]{1,0:T(8,128)(2,1)}, bf16[128,5120]{1,0:T(8,128)(2,1)}, u32[]{:S(2)}, u32[]{:S(2)}) collective-permute-start(bf16[128,5120]{1,0:T(8,128)(2,1)} %collective-permute-done.2), channel_id=1, source_target_pairs={{0,1},{1,2},{2,3},{3,4},{4,5},{5,6},{6,7},{7,8},{8,9},{9,10},{10,1... | collective-permute-start | bytes 3932168 | tf_op jit(solution)/shard_map/ppermute | solution.py:19
  74.1 42.7 %collective-permute-start.5 = (bf16[128,5120]{1,0:T(8,128)(2,1)}, bf16[128,5120]{1,0:T(8,128)(2,1)}, u32[]{:S(2)}, u32[]{:S(2)}) collective-permute-start(bf16[128,5120]{1,0:T(8,128)(2,1)} %collective-permute-done.3), channel_id=1, source_target_pairs={{0,15},{1,0},{2,1},{3,2},{4,3},{5,4},{6,5},{7,6},{8,7},{9,8},{10,9... | collective-permute-start | bytes 3932168 | tf_op jit(solution)/shard_map/ppermute | solution.py:22
  105.8 30.8 %collective-permute-start.6 = (bf16[128,5120]{1,0:T(8,128)(2,1)}, bf16[128,5120]{1,0:T(8,128)(2,1)}, u32[]{:S(2)}, u32[]{:S(2)}) collective-permute-start(bf16[128,5120]{1,0:T(8,128)(2,1)} %collective-permute-done.4), channel_id=1, source_target_pairs={{0,1},{1,2},{2,3},{3,4},{4,5},{5,6},{6,7},{7,8},{8,9},{9,10},{10,1... | collective-permute-start | bytes 3932168 | tf_op jit(solution)/shard_map/ppermute | solution.py:19
  116.8 29.8 %collective-permute-start.7 = (bf16[128,5120]{1,0:T(8,128)(2,1)}, bf16[128,5120]{1,0:T(8,128)(2,1)S(1)}, u32[]{:S(2)}, u32[]{:S(2)}) collective-permute-start(bf16[128,5120]{1,0:T(8,128)(2,1)} %collective-permute-done.5), channel_id=1, source_target_pairs={{0,15},{1,0},{2,1},{3,2},{4,3},{5,4},{6,5},{7,6},{8,7},{9,8},{10,9... | collective-permute-start | bytes 3932168 | tf_op jit(solution)/shard_map/ppermute | solution.py:22
  136.6 29.8 %collective-permute-start.8 = (bf16[128,5120]{1,0:T(8,128)(2,1)}, bf16[128,5120]{1,0:T(8,128)(2,1)S(1)}, u32[]{:S(2)}, u32[]{:S(2)}) collective-permute-start(bf16[128,5120]{1,0:T(8,128)(2,1)} %collective-permute-done.6), channel_id=1, source_target_pairs={{0,1},{1,2},{2,3},{3,4},{4,5},{5,6},{6,7},{7,8},{8,9},{9,10},{10,1... | collective-permute-start | bytes 3932168 | tf_op jit(solution)/shard_map/ppermute | solution.py:19
  146.6 29.2 %collective-permute-start.9 = (bf16[128,5120]{1,0:T(8,128)(2,1)S(1)}, bf16[128,5120]{1,0:T(8,128)(2,1)S(1)}, u32[]{:S(2)}, u32[]{:S(2)}) collective-permute-start(bf16[128,5120]{1,0:T(8,128)(2,1)S(1)} %collective-permute-done.7), channel_id=1, source_target_pairs={{0,15},{1,0},{2,1},{3,2},{4,3},{5,4},{6,5},{7,6},{8,7},{9,8},{10,9... | collective-permute-start | bytes 3932168 | tf_op jit(solution)/shard_map/ppermute | solution.py:22
  166.4 28.6 %collective-permute-start.10 = (bf16[128,5120]{1,0:T(8,128)(2,1)S(1)}, bf16[128,5120]{1,0:T(8,128)(2,1)S(1)}, u32[]{:S(2)}, u32[]{:S(2)}) collective-permute-start(bf16[128,5120]{1,0:T(8,128)(2,1)S(1)} %collective-permute-done.8), channel_id=1, source_target_pairs={{0,1},{1,2},{2,3},{3,4},{4,5},{5,6},{6,7},{7,8},{8,9},{9,10},{10,1... | collective-permute-start | bytes 3932168 | tf_op jit(solution)/shard_map/ppermute | solution.py:19
  175.8 28.3 %collective-permute-start.11 = (bf16[128,5120]{1,0:T(8,128)(2,1)S(1)}, bf16[128,5120]{1,0:T(8,128)(2,1)S(1)}, u32[]{:S(2)}, u32[]{:S(2)}) collective-permute-start(bf16[128,5120]{1,0:T(8,128)(2,1)S(1)} %collective-permute-done.9), channel_id=1, source_target_pairs={{0,15},{1,0},{2,1},{3,2},{4,3},{5,4},{6,5},{7,6},{8,7},{9,8},{10,9... | collective-permute-start | bytes 3932168 | tf_op jit(solution)/shard_map/ppermute | solution.py:22
  195.0 27.7 %collective-permute-start.12 = (bf16[128,5120]{1,0:T(8,128)(2,1)S(1)}, bf16[128,5120]{1,0:T(8,128)(2,1)S(1)}, u32[]{:S(2)}, u32[]{:S(2)}) collective-permute-start(bf16[128,5120]{1,0:T(8,128)(2,1)S(1)} %collective-permute-done.10), channel_id=1, source_target_pairs={{0,1},{1,2},{2,3},{3,4},{4,5},{5,6},{6,7},{7,8},{8,9},{9,10},{10,1... | collective-permute-start | bytes 3932168 | tf_op jit(solution)/shard_map/ppermute | solution.py:19
  204.1 27.4 %collective-permute-start.13 = (bf16[128,5120]{1,0:T(8,128)(2,1)S(1)}, bf16[128,5120]{1,0:T(8,128)(2,1)S(1)}, u32[]{:S(2)}, u32[]{:S(2)}) collective-permute-start(bf16[128,5120]{1,0:T(8,128)(2,1)S(1)} %collective-permute-done.11), channel_id=1, source_target_pairs={{0,15},{1,0},{2,1},{3,2},{4,3},{5,4},{6,5},{7,6},{8,7},{9,8},{10,9... | collective-permute-start | bytes 3932168 | tf_op jit(solution)/shard_map/ppermute | solution.py:22
  222.7 27.2 %collective-permute-start.14 = (bf16[128,5120]{1,0:T(8,128)(2,1)S(1)}, bf16[128,5120]{1,0:T(8,128)(2,1)S(1)}, u32[]{:S(2)}, u32[]{:S(2)}) collective-permute-start(bf16[128,5120]{1,0:T(8,128)(2,1)S(1)} %collective-permute-done.12), channel_id=1, source_target_pairs={{0,1},{1,2},{2,3},{3,4},{4,5},{5,6},{6,7},{7,8},{8,9},{9,10},{10,1... | collective-permute-start | bytes 3932168 | tf_op jit(solution)/shard_map/ppermute | solution.py:19
  251.1 15.5 %copy-start.5 = (f32[8]{0:T(128)S(1)}, f32[8]{0:T(128)}, u32[]{:S(2)}) copy-start(f32[8]{0:T(128)} %param.15) | copy-start | bytes 100
  251.1 61.1 %copy-start.1 = (f32[640,320]{0,1:T(8,128)S(1)}, f32[640,320]{0,1:T(8,128)}, u32[]{:S(2)}) copy-start(f32[640,320]{0,1:T(8,128)} %param.10) | copy-start | bytes 2457604
  265.1 145.4 %all-gather.2.cloned.1.call-start = ((), (), s32[]{:S(2)}) async-start(), calls=%async_computation.2 | async-start | bytes 3686400 | tf_op jit(solution)/shard_map/all_gather | solution.py:64
Sparse Core Ops, SparseCore 0:
  265.2 46.9 reduce-scatter.1
  385.0 25.4 all-gather.1
